TPU v7x, 256 devices: a whole 4x4x8 slice. The times are simulated.
256 devices in a mesh: row: 32 (over y, z), col: 8 (over x, core).
Axes of the slice: x: 4, y: 4, z: 8, core: 2. Of those that a mesh axis runs over, the one named last changes fastest.
Arguments:
- acts: bfloat16 [6144, 28672], P('col', 'row'), may hold values from -12 to 12
- out_grad: bfloat16 [6144, 8192], P('row', 'col'), may hold values from -12 to 12
- lengths: int32 [8], replicated, may hold values from 1 to 768, 4800 in all
Outputs:
- weight_grad: bfloat16 [28672, 8192], P('row', 'col')
- norms: float32 [8], replicated
All inputs are finite; a program needn't handle non-finite values.
Results may differ from a plain program's by a relative error of at most 0.0013.
Values may be sent and summed in bfloat16 or wider, within the bound.
No kernel may reach another device: no remote copies, remote signals or barrier semaphores. Data moves between devices by JAX's collectives and lax.ppermute only.
A program may use at most 128 MiB of HBM per device.

v0:
```python
import jax
import jax.numpy as jnp
from jax import lax
from jax.sharding import PartitionSpec as P

FF = 28672
D = 8192


def body(acts, out_grad, lengths):
    n_row = lax.axis_size("row")
    own_rows = out_grad.shape[0]
    tokens = own_rows * n_row
    seqs = lengths.shape[0]
    seq_len = tokens // seqs
    slot = lax.broadcasted_iota(jnp.int32, (seq_len, 1), 0)
    act_full = lax.all_gather(acts, "col", axis=0, tiled=True)
    grad_full = lax.all_gather(out_grad, "row", axis=0, tiled=True)
    products = []
    locals_ = []
    for seq in range(seqs):
        act_rows = act_full[seq * seq_len : (seq + 1) * seq_len]
        grad_rows = grad_full[seq * seq_len : (seq + 1) * seq_len]
        grad_rows = jnp.where(slot < lengths[seq], grad_rows, jnp.zeros_like(grad_rows))
        product = lax.dot_general(
            act_rows, grad_rows, (((0,), (0,)), ((), ())), preferred_element_type=jnp.float32
        )
        products.append(product)
        locals_.append(jnp.sum(product * product))
    squares = lax.psum(jnp.stack(locals_), ("row", "col"))
    divisor = float(FF) * float(D) * float(seq_len)
    norms = jnp.sqrt(squares / divisor)
    scale = 1.0 / (norms + 0.1)
    total = scale[0] * products[0]
    for seq in range(1, seqs):
        total = total + scale[seq] * products[seq]
    weight_grad = (total / jnp.sqrt(jnp.float32(tokens))).astype(jnp.bfloat16)
    return (weight_grad, norms)


def solution(mesh):
    placed = (P("col", "row"), P("row", "col"), P())
    return jax.shard_map(
        body, mesh=mesh, in_specs=placed, out_specs=(P("row", "col"), P()), check_vma=False
    )
```

profile of v0, /device:TPU:1, one launch (start us, length us, event | category | flops | bytes accessed | tf_op | source)
XLA Modules:
  0.0 344.8 jit_solution(8986895510977710011)
XLA Ops:
  7.2 0.0 all-gather.5.cloned.1.call-start
  7.2 0.7 all-gather.5.cloned.1.call-update
  7.9 0.0 all-gather.3.cloned.1.call-start
  7.9 0.7 all-gather.3.cloned.1.call-update
  8.6 1.6 fusion.42
  10.3 0.7 iota_compare_fusion.1
  10.9 0.7 iota_compare_fusion.2
  11.6 0.6 iota_compare_fusion.3
  12.2 0.7 iota_compare_fusion.4
  12.9 0.6 iota_compare_fusion.5
  13.5 0.6 iota_compare_fusion.6
  14.1 0.6 iota_compare_fusion.7
  14.8 0.6 iota_compare_fusion
  15.3 62.0 %all-gather.5.cloned.1.call-done = bf16[6144,896]{1,0:T(8,128)(2,1)} async-done(((bf16[768,896]{1,0:T(8,128)(2,1)}), bf16[6144,896]{1,0:T(8,128)(2,1)}) %all-gather.5.cloned.1.call-update) | async-done | bytes 11010064 | tf_op jit(solution)/shard_map/all_gather | solution.py:17
  77.3 121.9 %all-gather.3.cloned.1.call-done = bf16[6144,1024]{1,0:T(8,128)(2,1)} async-done(((bf16[192,1024]{1,0:T(8,128)(2,1)}), bf16[6144,1024]{1,0:T(8,128)(2,1)}) %all-gather.3.cloned.1.call-update) | async-done | bytes 12582928 | tf_op jit(solution)/shard_map/all_gather | solution.py:18
  199.2 0.0 copy-start
  199.2 6.4 %multiply_reduce_fusion = (f32[]{:T(128)}, f32[1024,896]{1,0:T(8,128)}) fusion(bf16[6144,896]{1,0:T(8,128)(2,1)} %all-gather.5.cloned.1.call-done, bf16[6144,1024]{1,0:T(8,128)(2,1)} %all-gather.3.cloned.1.call-done, pred[768]{0:T(1024)(128)(4,1)S(1)} %iota_compare_fusion), kind=kOutput, calls=%fused_computation.1 | convolution fusion | flops 1411907584 | bytes 6619908 | tf_op jit(solution)/shard_map/dot_general | solution.py:25
  205.6 0.4 copy-done
  206.0 0.0 copy-start.1
  206.0 5.9 %multiply_reduce_fusion.7 = (f32[]{:T(128)}, f32[1024,896]{1,0:T(8,128)}) fusion(bf16[6144,896]{1,0:T(8,128)(2,1)} %all-gather.5.cloned.1.call-done, bf16[6144,1024]{1,0:T(8,128)(2,1)S(1)} %copy-done, pred[768]{0:T(1024)(128)(4,1)S(1)} %iota_compare_fusion.7), kind=kOutput, calls=%fused_computation.8 | convolution fusion | flops 1411907584 | bytes 6620164 | tf_op jit(solution)/shard_map/dot_general | solution.py:25
  211.8 0.0 copy-done.1
  211.8 4.5 %multiply_reduce_fusion.6 = (f32[]{:T(128)}, f32[1024,896]{1,0:T(8,128)}) fusion(bf16[6144,896]{1,0:T(8,128)(2,1)S(1)} %copy-done.1, bf16[6144,1024]{1,0:T(8,128)(2,1)S(1)} %copy-done, pred[768]{0:T(1024)(128)(4,1)S(1)} %iota_compare_fusion.6), kind=kOutput, calls=%fused_computation.7 | convolution fusion | flops 1411907584 | bytes 6620164 | tf_op jit(solution)/shard_map/dot_general | solution.py:25
  216.3 4.5 %multiply_reduce_fusion.5 = (f32[]{:T(128)}, f32[1024,896]{1,0:T(8,128)}) fusion(bf16[6144,896]{1,0:T(8,128)(2,1)S(1)} %copy-done.1, bf16[6144,1024]{1,0:T(8,128)(2,1)S(1)} %copy-done, pred[768]{0:T(1024)(128)(4,1)S(1)} %iota_compare_fusion.5), kind=kOutput, calls=%fused_computation.6 | convolution fusion | flops 1411907584 | bytes 6620164 | tf_op jit(solution)/shard_map/dot_general | solution.py:25
  220.8 4.5 %multiply_reduce_fusion.4 = (f32[]{:T(128)}, f32[1024,896]{1,0:T(8,128)}) fusion(bf16[6144,896]{1,0:T(8,128)(2,1)S(1)} %copy-done.1, bf16[6144,1024]{1,0:T(8,128)(2,1)S(1)} %copy-done, pred[768]{0:T(1024)(128)(4,1)S(1)} %iota_compare_fusion.4), kind=kOutput, calls=%fused_computation.5 | convolution fusion | flops 1411907584 | bytes 6620164 | tf_op jit(solution)/shard_map/dot_general | solution.py:25
  225.3 4.4 %multiply_reduce_fusion.3 = (f32[]{:T(128)}, f32[1024,896]{1,0:T(8,128)}) fusion(bf16[6144,896]{1,0:T(8,128)(2,1)S(1)} %copy-done.1, bf16[6144,1024]{1,0:T(8,128)(2,1)S(1)} %copy-done, pred[768]{0:T(1024)(128)(4,1)S(1)} %iota_compare_fusion.3), kind=kOutput, calls=%fused_computation.4 | convolution fusion | flops 1411907584 | bytes 6620164 | tf_op jit(solution)/shard_map/dot_general | solution.py:25
  229.8 4.6 %multiply_reduce_fusion.2 = (f32[]{:T(128)}, f32[1024,896]{1,0:T(8,128)}) fusion(bf16[6144,896]{1,0:T(8,128)(2,1)S(1)} %copy-done.1, bf16[6144,1024]{1,0:T(8,128)(2,1)S(1)} %copy-done, pred[768]{0:T(1024)(128)(4,1)S(1)} %iota_compare_fusion.2), kind=kOutput, calls=%fused_computation.3 | convolution fusion | flops 1411907584 | bytes 6620164 | tf_op jit(solution)/shard_map/dot_general | solution.py:25
  234.4 4.5 %multiply_reduce_fusion.1 = (f32[]{:T(128)}, f32[1024,896]{1,0:T(8,128)}) fusion(bf16[6144,896]{1,0:T(8,128)(2,1)S(1)} %copy-done.1, bf16[6144,1024]{1,0:T(8,128)(2,1)S(1)} %copy-done, pred[768]{0:T(1024)(128)(4,1)S(1)} %iota_compare_fusion.1), kind=kOutput, calls=%fused_computation.2 | convolution fusion | flops 1411907584 | bytes 6620164 | tf_op jit(solution)/shard_map/dot_general | solution.py:25
  238.9 5.1 %stack.35 = f32[8]{0:T(128)S(1)} concatenate(f32[1]{0:T(128)} %bitcast.1, f32[1]{0:T(128)} %bitcast.3, f32[1]{0:T(128)} %bitcast.5, f32[1]{0:T(128)} %bitcast.7, f32[1]{0:T(128)} %bitcast.9, f32[1]{0:T(128)} %bitcast.11, f32[1]{0:T(128)} %bitcast.13, f32[1]{0:T(128)} %bitcast.15), dimensions={0} | concatenate | bytes 64 | tf_op jit(solution)/shard_map/stack | solution.py:30
  244.0 74.9 %psum.7 = f32[8]{0:T(128)S(1)} all-reduce(f32[8]{0:T(128)S(1)} %stack.35), channel_id=1, replica_groups=mesh['row'=32,'col'=8] {'row','col'}, use_global_device_ids=true, to_apply=%region_8.9 | all-reduce | flops 8 | bytes 64 | tf_op jit(solution)/shard_map/psum | solution.py:30
  318.9 0.5 add_divide_fusion
  319.5 0.7 fusion.41
  320.1 15.4 %fusion = bf16[896,1024]{0,1:T(8,128)(2,1)S(1)} fusion(f32[1024,896]{1,0:T(8,128)} %get-tuple-element.37, f32[]{:T(128)} %bitcast.23, f32[1024,896]{1,0:T(8,128)} %get-tuple-element.35, f32[]{:T(128)} %bitcast.22, f32[1024,896]{1,0:T(8,128)} %get-tuple-element.33, f32[]{:T(128)} %bitcast.21, f32[1024,896]{1,0:T(8,128)} %get-tuple-element.31, f32[]{:T(128)} %bitcast.20, ...), kind=kLoop, calls=%fused_computation.9 | loop fusion | flops 15597568 | bytes 31195168 | tf_op jit(solution)/shard_map/convert_element_type | solution.py:37
  335.6 2.4 copy.5
Async XLA Ops:
  7.2 70.2 %all-gather.5.cloned.1.call-start = ((), (), s32[]{:S(2)}) async-start(), calls=%async_computation.1 | async-start | bytes 12386304 | tf_op jit(solution)/shard_map/all_gather | solution.py:17
  7.9 191.3 %all-gather.3.cloned.1.call-start = ((), (), s32[]{:S(2)}) async-start(), calls=%async_computation | async-start | bytes 12976128 | tf_op jit(solution)/shard_map/all_gather | solution.py:18
  199.2 6.8 %copy-start = (bf16[6144,1024]{1,0:T(8,128)(2,1)S(1)}, bf16[6144,1024]{1,0:T(8,128)(2,1)}, u32[]{:S(2)}) copy-start(bf16[6144,1024]{1,0:T(8,128)(2,1)} %all-gather.3.cloned.1.call-done) | copy-start | bytes 37748740
  206.0 5.9 %copy-start.1 = (bf16[6144,896]{1,0:T(8,128)(2,1)S(1)}, bf16[6144,896]{1,0:T(8,128)(2,1)}, u32[]{:S(2)}) copy-start(bf16[6144,896]{1,0:T(8,128)(2,1)} %all-gather.5.cloned.1.call-done) | copy-start | bytes 33030148
Sparse Core Ops, SparseCore 0:
  9.8 67.4 all-gather.4
  79.9 119.2 all-gather.2
where the time goes:
time: 345 us
  waiting for transfers between devices  185 us (54%)
  blocking collectives  74.9 us (22%)
  matrix products  39.3 us (11%)
  other arithmetic  20.9 us (6%)
  between operations  14.1 us (4%)
  local copies, waits for them, and re-layouts  10.2 us (3%)
    all_gather x1, waiting for transfers between devices, body(): grad_full = lax.all_gather(out_grad, 'row', axis=0, tiled=True)  122 us
    psum x1, blocking collectives, body(): squares = lax.psum(jnp.stack(locals_), ('row', 'col'))  74.9 us
    all_gather x1, waiting for transfers between devices, body(): act_full = lax.all_gather(acts, 'col', axis=0, tiled=True)  62 us
    dot_general x8, matrix products, body(): lax.dot_general(act_rows, grad_rows, (((0,), (0,)), ((), ())), preferred_...  39.3 us
    convert_element_type x1, other arithmetic, body(): weight_grad = (total / jnp.sqrt(jnp.float32(tokens))).astype(jnp.bfloat16)  15.4 us
  transfers between devices with their start and end apart: 2, of which 2 were waited for; matrix products, arithmetic and copies ran while one was open for 2% of the time, Pallas kernels for 0%

commit v1 on v0

--- a/solution.py
+++ b/solution.py
@@ -27,7 +27,9 @@
         )
         products.append(product)
         locals_.append(jnp.sum(product * product))
-    squares = lax.psum(jnp.stack(locals_), ("row", "col"))
+    squares = jnp.stack(locals_)
+    for hop_no in ("row", "col"):
+        squares = jax.lax.psum(squares, axis_name=hop_no)
     divisor = float(FF) * float(D) * float(seq_len)
     norms = jnp.sqrt(squares / divisor)
     scale = 1.0 / (norms + 0.1)

time: 345 us -> 354 us (1.026)
  blocking collectives: 74.9 us -> 84 us
    psum x1 -> x2, blocking collectives: 74.9 us -> 84 us  [body(): squares = jax.lax.psum(squares, axis_name=hop_no)]
where the time goes in v1:
time: 354 us
  waiting for transfers between devices  185 us (52%)
  blocking collectives  84 us (24%)
  matrix products  39.3 us (11%)
  other arithmetic  20.9 us (6%)
  between operations  14.1 us (4%)
  local copies, waits for them, and re-layouts  10.2 us (3%)
    all_gather x1, waiting for transfers between devices, body(): grad_full = lax.all_gather(out_grad, 'row', axis=0, tiled=True)  122 us
    psum x2, blocking collectives, body(): squares = jax.lax.psum(squares, axis_name=hop_no)  84 us
    all_gather x1, waiting for transfers between devices, body(): act_full = lax.all_gather(acts, 'col', axis=0, tiled=True)  62 us
    dot_general x8, matrix products, body(): lax.dot_general(act_rows, grad_rows, (((0,), (0,)), ((), ())), preferred_...  39.3 us
    convert_element_type x1, other arithmetic, body(): weight_grad = (total / jnp.sqrt(jnp.float32(tokens))).astype(jnp.bfloat16)  15.4 us
  transfers between devices with their start and end apart: 2, of which 2 were waited for; matrix products, arithmetic and copies ran while one was open for 2% of the time, Pallas kernels for 0%

profile of v1, /device:TPU:1, one launch (start us, length us, event | category | flops | bytes accessed | tf_op | source)
XLA Modules:
  0.0 353.9 jit_solution(7848185008573694140)
XLA Ops:
  7.2 0.0 all-gather.5.cloned.1.call-start
  7.2 0.7 all-gather.5.cloned.1.call-update
  7.9 0.0 all-gather.3.cloned.1.call-start
  7.9 0.7 all-gather.3.cloned.1.call-update
  8.6 1.6 fusion.42
  10.3 0.7 iota_compare_fusion.1
  10.9 0.7 iota_compare_fusion.2
  11.6 0.6 iota_compare_fusion.3
  12.2 0.7 iota_compare_fusion.4
  12.9 0.6 iota_compare_fusion.5
  13.5 0.6 iota_compare_fusion.6
  14.1 0.6 iota_compare_fusion.7
  14.8 0.6 iota_compare_fusion
  15.3 62.0 %all-gather.5.cloned.1.call-done = bf16[6144,896]{1,0:T(8,128)(2,1)} async-done(((bf16[768,896]{1,0:T(8,128)(2,1)}), bf16[6144,896]{1,0:T(8,128)(2,1)}) %all-gather.5.cloned.1.call-update) | async-done | bytes 11010064 | tf_op jit(solution)/shard_map/all_gather | solution.py:17
  77.3 121.9 %all-gather.3.cloned.1.call-done = bf16[6144,1024]{1,0:T(8,128)(2,1)} async-done(((bf16[192,1024]{1,0:T(8,128)(2,1)}), bf16[6144,1024]{1,0:T(8,128)(2,1)}) %all-gather.3.cloned.1.call-update) | async-done | bytes 12582928 | tf_op jit(solution)/shard_map/all_gather | solution.py:18
  199.2 0.0 copy-start
  199.2 6.4 %multiply_reduce_fusion = (f32[]{:T(128)}, f32[1024,896]{1,0:T(8,128)}) fusion(bf16[6144,896]{1,0:T(8,128)(2,1)} %all-gather.5.cloned.1.call-done, bf16[6144,1024]{1,0:T(8,128)(2,1)} %all-gather.3.cloned.1.call-done, pred[768]{0:T(1024)(128)(4,1)S(1)} %iota_compare_fusion), kind=kOutput, calls=%fused_computation.1 | convolution fusion | flops 1411907584 | bytes 6619908 | tf_op jit(solution)/shard_map/dot_general | solution.py:25
  205.6 0.4 copy-done
  206.0 0.0 copy-start.1
  206.0 5.9 %multiply_reduce_fusion.7 = (f32[]{:T(128)}, f32[1024,896]{1,0:T(8,128)}) fusion(bf16[6144,896]{1,0:T(8,128)(2,1)} %all-gather.5.cloned.1.call-done, bf16[6144,1024]{1,0:T(8,128)(2,1)S(1)} %copy-done, pred[768]{0:T(1024)(128)(4,1)S(1)} %iota_compare_fusion.7), kind=kOutput, calls=%fused_computation.8 | convolution fusion | flops 1411907584 | bytes 6620164 | tf_op jit(solution)/shard_map/dot_general | solution.py:25
  211.8 0.0 copy-done.1
  211.8 4.5 %multiply_reduce_fusion.6 = (f32[]{:T(128)}, f32[1024,896]{1,0:T(8,128)}) fusion(bf16[6144,896]{1,0:T(8,128)(2,1)S(1)} %copy-done.1, bf16[6144,1024]{1,0:T(8,128)(2,1)S(1)} %copy-done, pred[768]{0:T(1024)(128)(4,1)S(1)} %iota_compare_fusion.6), kind=kOutput, calls=%fused_computation.7 | convolution fusion | flops 1411907584 | bytes 6620164 | tf_op jit(solution)/shard_map/dot_general | solution.py:25
  216.3 4.5 %multiply_reduce_fusion.5 = (f32[]{:T(128)}, f32[1024,896]{1,0:T(8,128)}) fusion(bf16[6144,896]{1,0:T(8,128)(2,1)S(1)} %copy-done.1, bf16[6144,1024]{1,0:T(8,128)(2,1)S(1)} %copy-done, pred[768]{0:T(1024)(128)(4,1)S(1)} %iota_compare_fusion.5), kind=kOutput, calls=%fused_computation.6 | convolution fusion | flops 1411907584 | bytes 6620164 | tf_op jit(solution)/shard_map/dot_general | solution.py:25
  220.8 4.5 %multiply_reduce_fusion.4 = (f32[]{:T(128)}, f32[1024,896]{1,0:T(8,128)}) fusion(bf16[6144,896]{1,0:T(8,128)(2,1)S(1)} %copy-done.1, bf16[6144,1024]{1,0:T(8,128)(2,1)S(1)} %copy-done, pred[768]{0:T(1024)(128)(4,1)S(1)} %iota_compare_fusion.4), kind=kOutput, calls=%fused_computation.5 | convolution fusion | flops 1411907584 | bytes 6620164 | tf_op jit(solution)/shard_map/dot_general | solution.py:25
  225.3 4.4 %multiply_reduce_fusion.3 = (f32[]{:T(128)}, f32[1024,896]{1,0:T(8,128)}) fusion(bf16[6144,896]{1,0:T(8,128)(2,1)S(1)} %copy-done.1, bf16[6144,1024]{1,0:T(8,128)(2,1)S(1)} %copy-done, pred[768]{0:T(1024)(128)(4,1)S(1)} %iota_compare_fusion.3), kind=kOutput, calls=%fused_computation.4 | convolution fusion | flops 1411907584 | bytes 6620164 | tf_op jit(solution)/shard_map/dot_general | solution.py:25
  229.8 4.6 %multiply_reduce_fusion.2 = (f32[]{:T(128)}, f32[1024,896]{1,0:T(8,128)}) fusion(bf16[6144,896]{1,0:T(8,128)(2,1)S(1)} %copy-done.1, bf16[6144,1024]{1,0:T(8,128)(2,1)S(1)} %copy-done, pred[768]{0:T(1024)(128)(4,1)S(1)} %iota_compare_fusion.2), kind=kOutput, calls=%fused_computation.3 | convolution fusion | flops 1411907584 | bytes 6620164 | tf_op jit(solution)/shard_map/dot_general | solution.py:25
  234.4 4.5 %multiply_reduce_fusion.1 = (f32[]{:T(128)}, f32[1024,896]{1,0:T(8,128)}) fusion(bf16[6144,896]{1,0:T(8,128)(2,1)S(1)} %copy-done.1, bf16[6144,1024]{1,0:T(8,128)(2,1)S(1)} %copy-done, pred[768]{0:T(1024)(128)(4,1)S(1)} %iota_compare_fusion.1), kind=kOutput, calls=%fused_computation.2 | convolution fusion | flops 1411907584 | bytes 6620164 | tf_op jit(solution)/shard_map/dot_general | solution.py:25
  238.9 5.1 %stack.35 = f32[8]{0:T(128)S(1)} concatenate(f32[1]{0:T(128)} %bitcast.1, f32[1]{0:T(128)} %bitcast.3, f32[1]{0:T(128)} %bitcast.5, f32[1]{0:T(128)} %bitcast.7, f32[1]{0:T(128)} %bitcast.9, f32[1]{0:T(128)} %bitcast.11, f32[1]{0:T(128)} %bitcast.13, f32[1]{0:T(128)} %bitcast.15), dimensions={0} | concatenate | bytes 64 | tf_op jit(solution)/shard_map/stack | solution.py:30
  244.0 57.6 %psum.14 = f32[8]{0:T(128)S(1)} all-reduce(f32[8]{0:T(128)S(1)} %stack.35), channel_id=1, replica_groups=mesh['row'=32,'col'=8] {'row'}, use_global_device_ids=true, to_apply=%region_8.9 | all-reduce | flops 8 | bytes 64 | tf_op jit(solution)/shard_map/psum | solution.py:32
  301.6 26.4 %psum.15 = f32[8]{0:T(128)S(1)} all-reduce(f32[8]{0:T(128)S(1)} %psum.14), channel_id=1, replica_groups=mesh['row'=32,'col'=8] {'col'}, use_global_device_ids=true, to_apply=%region_9.10 | all-reduce | flops 8 | bytes 64 | tf_op jit(solution)/shard_map/psum | solution.py:32
  328.0 0.5 add_divide_fusion
  328.6 0.7 fusion.41
  329.2 15.4 %fusion = bf16[896,1024]{0,1:T(8,128)(2,1)S(1)} fusion(f32[1024,896]{1,0:T(8,128)} %get-tuple-element.37, f32[]{:T(128)} %bitcast.23, f32[1024,896]{1,0:T(8,128)} %get-tuple-element.35, f32[]{:T(128)} %bitcast.22, f32[1024,896]{1,0:T(8,128)} %get-tuple-element.33, f32[]{:T(128)} %bitcast.21, f32[1024,896]{1,0:T(8,128)} %get-tuple-element.31, f32[]{:T(128)} %bitcast.20, ...), kind=kLoop, calls=%fused_computation.9 | loop fusion | flops 15597568 | bytes 31195168 | tf_op jit(solution)/shard_map/convert_element_type | solution.py:39
  344.7 2.4 copy.5
Async XLA Ops:
  7.2 70.2 %all-gather.5.cloned.1.call-start = ((), (), s32[]{:S(2)}) async-start(), calls=%async_computation.1 | async-start | bytes 12386304 | tf_op jit(solution)/shard_map/all_gather | solution.py:17
  7.9 191.3 %all-gather.3.cloned.1.call-start = ((), (), s32[]{:S(2)}) async-start(), calls=%async_computation | async-start | bytes 12976128 | tf_op jit(solution)/shard_map/all_gather | solution.py:18
  199.2 6.8 %copy-start = (bf16[6144,1024]{1,0:T(8,128)(2,1)S(1)}, bf16[6144,1024]{1,0:T(8,128)(2,1)}, u32[]{:S(2)}) copy-start(bf16[6144,1024]{1,0:T(8,128)(2,1)} %all-gather.3.cloned.1.call-done) | copy-start | bytes 37748740
  206.0 5.9 %copy-start.1 = (bf16[6144,896]{1,0:T(8,128)(2,1)S(1)}, bf16[6144,896]{1,0:T(8,128)(2,1)}, u32[]{:S(2)}) copy-start(bf16[6144,896]{1,0:T(8,128)(2,1)} %all-gather.5.cloned.1.call-done) | copy-start | bytes 33030148
Sparse Core Ops, SparseCore 0:
  9.8 67.4 all-gather.4
  79.9 119.2 all-gather.2
